TPU v7x, 32 devices: a whole 2x2x4 slice. The times are simulated.
32 devices in a mesh: au: 8 (over z, core), vert: 4 (over y, x).
Axes of the slice: x: 2, y: 2, z: 4, core: 2. Of those that a mesh axis runs over, the one named last changes fastest.
Arguments:
- vis_value: float32 [128, 128, 2, 128], P('au', 'vert'), may hold values from -6 to 6
- vis_pos: int32 [128, 128, 2, 128], P('au', 'vert'), may hold values from 0 to 1048575, as said below
- counts: int32 [128, 128], P('au', 'vert'), may hold values from 21 to 128, as said below
- kernel: float32 [8, 128], replicated, may hold values from 0.05 to 0.5
Outputs:
- image: float32 [8192, 8192], P(('au', 'vert'))
Inputs may be any that keep to these rules, and one draw needn't show every extreme that they name: Slot k of patch (p, q) holds a visibility exactly when k < counts[p, q]; in every draw some patch has all 128 slots live. vis_pos[p, q, 0, k] lies in [p * 64 * 128, (p + 1) * 64 * 128) and vis_pos[p, q, 1, k] in [q * 64 * 128, (q + 1) * 64 * 128), in every slot.
All inputs are finite; a program needn't handle non-finite values.
Results may differ from a plain program's by a relative error of at most 0.0003.
Values sent between devices are 32-bit elements; how exact they have to be, the bound alone decides.
A program may use at most 192 MiB of HBM per device.

v0:
```python
import math

import jax
import jax.numpy as jnp
from jax import lax
from jax.sharding import PartitionSpec as P

PATCH = 64
PR = 128
PC = 128


highest = lax.Precision.HIGHEST


def passed_along(value, axis, steps):
    count = lax.axis_size(axis)
    initial, last = (max(0, -steps), min(count, count - steps))
    return lax.ppermute(value, axis, [(source, source + steps) for source in range(initial, last)])


def fourier(length):
    index_list = jnp.arange(length, dtype=jnp.int32)
    angles = (
        2.0
        * math.pi
        / length
        * (index_list[:, None] * index_list[None, :] % length).astype(jnp.float32)
    )
    return jnp.stack([jnp.cos(angles), jnp.sin(angles)])


def twiddle(outer_size, inner_size, length):
    row_index = jnp.arange(outer_size, dtype=jnp.int32)[:, None]
    col_index = jnp.arange(inner_size, dtype=jnp.int32)[None, :]
    angles = 2.0 * math.pi / length * (row_index * col_index % length).astype(jnp.float32)
    return (jnp.cos(angles), jnp.sin(angles))


def row_transform(row_field):
    row_count = row_field.shape[1]
    length = row_field.shape[2]
    inner_size = 128
    outer_size = length // inner_size
    first_table = fourier(outer_size)
    second_table = fourier(inner_size)
    turn_cos, turn_sin = twiddle(outer_size, inner_size, length)
    blocked = row_field.reshape(2, row_count, outer_size, inner_size)
    product = jnp.einsum("saq,crqp->scrap", first_table, blocked, precision=highest)
    real_part = product[0, 0] - product[1, 1]
    imag_part = product[0, 1] + product[1, 0]
    rotated = jnp.stack(
        [real_part * turn_cos - imag_part * turn_sin, real_part * turn_sin + imag_part * turn_cos]
    )
    product = jnp.einsum("sbp,crap->scrba", second_table, rotated, precision=highest)
    result = jnp.stack([product[0, 0] - product[1, 1], product[0, 1] + product[1, 0]])
    return result.reshape(2, row_count, length)


def column_transform(received, image_scale):
    length = received.shape[1]
    item_count = received.shape[3]
    inner_size = 128
    outer_size = length // inner_size
    first_table = fourier(outer_size)
    second_table = fourier(inner_size)
    turn_cos, turn_sin = twiddle(outer_size, inner_size, length)
    blocked = received.reshape(2, outer_size, inner_size, item_count)
    product = jnp.einsum("saq,cqpy->scapy", first_table, blocked, precision=highest)
    real_part = product[0, 0] - product[1, 1]
    imag_part = product[0, 1] + product[1, 0]
    rotated_real = real_part * turn_cos[..., None] - imag_part * turn_sin[..., None]
    rotated_imag = real_part * turn_sin[..., None] + imag_part * turn_cos[..., None]
    image_rows = jnp.einsum("bp,apy->yba", second_table[0], rotated_real, precision=highest)
    image_rows = image_rows - jnp.einsum(
        "bp,apy->yba", second_table[1], rotated_imag, precision=highest
    )
    return (image_rows * image_scale).reshape(item_count, length)


def patch_grid(values, positions, counts, kernel):
    kernel_width, oversample = kernel.shape
    cell_index = positions // oversample
    fine_index = positions - cell_index * oversample
    offsets = cell_index % PATCH
    selector = (fine_index[..., None] == jnp.arange(oversample, dtype=jnp.int32)).astype(
        jnp.float32
    )
    tap_values = jnp.einsum("nako,to->nakt", selector, kernel, precision=highest)
    slot_count = values.shape[2]
    live_mask = (jnp.arange(slot_count, dtype=jnp.int32)[None, :] < counts[:, None]).astype(
        jnp.float32
    )
    extent = PATCH + kernel_width
    distance = jnp.arange(extent, dtype=jnp.int32)[None, None, None, :] - offsets[..., None]
    weights = jnp.zeros(distance.shape, jnp.float32)
    for tap_step in range(kernel_width):
        weights = weights + jnp.where(
            distance == tap_step, tap_values[..., tap_step : tap_step + 1], 0.0
        )
    row_weights = weights[:, 0] * live_mask[:, :, None]
    scaled = values[:, :, :, None] * weights[:, 1][:, None]
    core_part = jnp.einsum("nki,nckj->nicj", row_weights, scaled[..., :PATCH], precision=highest)
    side_part = jnp.einsum("nki,nckj->ncji", row_weights, scaled[..., PATCH:], precision=highest)
    return (core_part, side_part)


def grid_block(values, positions, counts, kernel):
    kernel_width = kernel.shape[0]
    band_count = values.shape[0]
    column_count = values.shape[1]
    slot_count = values.shape[3]
    group_count = band_count * column_count // 32
    extent = PATCH + kernel_width

    def grid_group(members):
        return patch_grid(members[0], members[1], members[2], kernel)

    core_part, side_part = lax.map(
        grid_group,
        (
            values.reshape(group_count, 32, 2, slot_count),
            positions.reshape(group_count, 32, 2, slot_count),
            counts.reshape(group_count, 32),
        ),
    )
    core_part = core_part.reshape(band_count, column_count, extent, 2, PATCH)
    side_part = side_part.reshape(band_count, column_count, 2, kernel_width, extent)
    tile_field = core_part[:, :, :PATCH].transpose(3, 0, 2, 1, 4)
    lower_rows = core_part[:, :, PATCH:].transpose(3, 0, 2, 1, 4)
    tile_field = tile_field.at[:, 1:, :kernel_width].add(lower_rows[:, :-1])
    bottom_strip = lower_rows[:, -1]
    beside_cols = side_part[..., :PATCH].transpose(2, 0, 4, 1, 3)
    tile_field = tile_field.at[:, :, :, 1:, :kernel_width].add(beside_cols[:, :, :, :-1])
    right_strip = beside_cols[:, :, :, -1]
    diagonal = side_part[..., PATCH:].transpose(2, 0, 4, 1, 3)
    tile_field = tile_field.at[:, 1:, :kernel_width, 1:, :kernel_width].add(
        diagonal[:, :-1, :, :-1]
    )
    bottom_strip = bottom_strip.at[:, :, 1:, :kernel_width].add(diagonal[:, -1, :, :-1])
    right_strip = right_strip.at[:, 1:, :kernel_width].add(diagonal[:, :-1, :, -1])
    corner_block = diagonal[:, -1, :, -1]
    tile_field = tile_field.reshape(2, band_count * PATCH, column_count * PATCH)
    bottom_strip = bottom_strip.reshape(2, kernel_width, column_count * PATCH)
    right_strip = right_strip.reshape(2, band_count * PATCH, kernel_width)
    return (tile_field, bottom_strip, right_strip, corner_block)


def local(vis_value, vis_pos, counts, kernel):
    kernel_width = kernel.shape[0]
    device_count = lax.axis_size("au") * lax.axis_size("vert")
    slot_count = vis_value.shape[3]
    image_scale = 1.0 / math.sqrt(PR * PC * slot_count)
    vert_count = lax.axis_size("vert")
    band_count = vis_value.shape[0] // vert_count
    local_columns = vis_value.shape[1]
    moved_values = lax.all_to_all(
        vis_value.reshape(vert_count, band_count, local_columns, 2, slot_count),
        "vert",
        split_axis=0,
        concat_axis=2,
        tiled=True,
    )
    positions, tallies = (
        lax.all_to_all(
            vis_pos.reshape(vert_count, band_count, local_columns, 2, slot_count),
            "vert",
            split_axis=0,
            concat_axis=2,
            tiled=True,
        ),
        lax.all_to_all(
            counts.reshape(vert_count, band_count, local_columns),
            "vert",
            split_axis=0,
            concat_axis=2,
            tiled=True,
        ),
    )
    column_count = local_columns * vert_count
    tile_field, bottom_strip, right_strip, corner_block = grid_block(
        moved_values.reshape(band_count, column_count, 2, slot_count),
        positions.reshape(band_count, column_count, 2, slot_count),
        tallies.reshape(band_count, column_count),
        kernel,
    )
    arrived = passed_along(bottom_strip, ("au", "vert"), 1)
    tile_field = tile_field.at[:, :kernel_width].add(arrived)
    row_field = row_transform(tile_field)
    length = row_field.shape[2]
    column_share = length // device_count
    return column_transform(
        lax.all_to_all(
            row_field.reshape(2, row_field.shape[1], device_count, column_share),
            ("au", "vert"),
            split_axis=2,
            concat_axis=1,
            tiled=True,
        ),
        image_scale,
    )


def solution(mesh):
    in_specs = (P("au", "vert", None, None), P("au", "vert", None, None), P("au", "vert"), P())
    out_specs = P(("au", "vert"), None)
    return jax.shard_map(local, mesh=mesh, in_specs=in_specs, out_specs=out_specs, check_vma=False)
```

profile of v0, /device:TPU:0, one launch (start us, length us, event | category | flops | bytes accessed | tf_op | source)
XLA Modules:
  0.0 1479.7 jit_solution(16205292781377681390)
XLA Ops:
  1.4 5.2 all-to-all-start.1
  11.2 9.8 all_to_all.60
  31.0 218.0 %while.19 = (s32[]{:T(128)}, f32[16,32,72,2,64]{2,4,3,1,0:T(8,128)}, f32[16,32,2,8,72]{4,3,2,1,0:T(8,128)}, s32[16,32,2,128]{3,1,2,0:T(8,128)S(1)}, f32[8,128]{1...) while((s32[]{:T(128)}, f32[16,32,72,2,64]{2,4,3,1,0:T(8,128)}, ...), condition=%wide.region_1.2_spmd, body=%wide.region_0.1_spmd.sunk | while | flops 626892800 | bytes 24827360 | solution.py:119
  31.1 4.4 fusion.117
  44.7 4.4 fusion.117
  58.4 4.4 fusion.117
  72.0 4.4 fusion.117
  85.6 4.4 fusion.117
  99.3 4.4 fusion.117
  112.9 4.4 fusion.117
  126.5 4.4 fusion.117
  140.1 4.4 fusion.117
  153.7 4.4 fusion.117
  167.4 4.4 fusion.117
  181.0 4.4 fusion.117
  249.0 28.6 %slice.368 = f32[4,128,8,2,64]{2,4,3,1,0:T(8,128)} slice(f32[4,128,72,2,64]{2,4,3,1,0:T(8,128)} %bitcast.250), slice={[0:4], [0:128], [64:72], [0:2], [0:64]} | slice | bytes 4194304 | tf_op jit(solution)/shard_map/slice | solution.py:130
  280.9 8.5 slice.367
  289.4 20.7 %copy.145 = f32[4,128,8,2,64]{4,1,2,3,0:T(8,128)} copy(f32[4,128,8,2,64]{2,4,3,1,0:T(8,128)} %slice.368) | data formatting | bytes 4194304
  310.1 33.3 %copy.143 = f32[4,128,64,2,64]{4,1,2,3,0:T(8,128)} copy(f32[4,128,64,2,64]{2,4,3,1,0:T(8,128)} %bitcast.251) | data formatting | bytes 33554432
  343.5 14.8 copy.144
  358.3 5.3 slice.374
  363.6 26.6 %copy.146 = f32[4,128,2,8,64]{3,1,4,2,0:T(8,128)} copy(f32[4,128,2,8,64]{4,3,2,1,0:T(8,128)} %bitcast.208) | data formatting | bytes 4194304
  390.2 5.5 copy.147
  400.7 8.9 scatter-add.21
  420.1 33.1 %slice_add_fusion = f32[2,4,64,127,8]{4,3,2,0,1:T(8,128)} fusion(f32[2,4,64,128,8]{4,3,2,0,1:T(8,128)} %bitcast.255, f32[2,4,64,128,64]{4,3,2,0,1:T(8,128)} %fusion.47), kind=kLoop, calls=%fused_computation.47 | loop fusion | flops 520192 | bytes 6242304 | tf_op jit(solution)/shard_map/add | solution.py:134
  453.2 270.0 %scatter-add.19 = f32[2,4,64,128,64]{4,3,2,0,1:T(8,128)} dynamic-update-slice(f32[2,4,64,128,64]{4,3,2,0,1:T(8,128)} %fusion.47, f32[2,4,64,127,8]{4,3,2,0,1:T(8,128)} %slice_add_fusion, s32[]{:T(128)} %constant.313.clone.1, s32[]{:T(128)} %constant.313.clone.1, s32[]{:T(128)} %constant.313.clone.1, s32[]{:T(128)} %constant.315.clone.1, s32[]{:T(128)} %constant.313.clone.1) | dynamic-update-slice | bytes 4161540 | tf_op jit(solution)/shard_map/scatter-add | solution.py:134
  726.6 23.2 %scatter-add.20 = f32[2,4,64,128,64]{4,3,2,0,1:T(8,128)} dynamic-update-slice(f32[2,4,64,128,64]{4,3,2,0,1:T(8,128)} %scatter-add.19, f32[2,3,8,127,8]{4,3,2,0,1:T(8,128)S(1)} %slice_add_fusion.4, s32[]{:T(128)} %constant.313.clone.1, s32[]{:T(128)} %constant.315.clone.1, s32[]{:T(128)} %constant.313.clone.1, s32[]{:T(128)} %constant.315.clone.1, s32[]{:T(128)} %constant.313.clone.1) | dynamic-update-slice | bytes 390148 | tf_op jit(solution)/shard_map/scatter-add | solution.py:137
  749.9 23.0 %copy.114 = f32[2,4,64,128,64]{4,3,2,1,0:T(8,128)} copy(f32[2,4,64,128,64]{4,3,2,0,1:T(8,128)} %scatter-add.20) | data formatting | bytes 33554432 | tf_op jit(solution)/shard_map/scatter-add | solution.py:137
  772.9 27.9 %reshape.663 = f32[2,256,8192]{2,1,0:T(8,128)} reshape(f32[2,4,64,128,64]{4,3,2,1,0:T(8,128)} %copy.114) | data formatting | bytes 33554432 | tf_op jit(solution)/shard_map/reshape | solution.py:143
  802.8 9.4 copy.152
  812.3 30.2 %convolution_bitcast_fusion = f32[2,2,256,64,128]{4,3,0,2,1:T(8,128)} fusion(f32[2,256,64,128,1]{3,2,1,0,4:T(8,128)S(1)} %bitcast.256, f32[1,64,64]{2,1,0:T(8,128)S(1)} %copy-done.2, f32[1,64,64]{2,1,0:T(8,128)S(1)} %copy-done.3), kind=kOutput, calls=%fused_computation.48 | convolution fusion | flops 6442459136 | bytes 50364416 | tf_op jit(solution)/shard_map/saq,crqp->scrap/dot_general | solution.py:49
  842.5 29.3 %multiply_subtract_fusion.1 = (f32[1,256,64,128]{3,2,1,0:T(8,128)}, f32[1,256,64,128]{3,2,1,0:T(8,128)}) fusion(f32[64,128]{1,0:T(8,128)S(1)} %copy-done.4, f32[64,128]{1,0:T(8,128)S(1)} %copy-done.5, f32[2,2,256,64,128]{4,3,0,2,1:T(8,128)} %convolution_bitcast_fusion), kind=kLoop, calls=%fused_computation.78 | loop fusion | flops 16777216 | bytes 50397184 | tf_op jit(solution)/shard_map/sub | solution.py:53
  871.8 11.9 maximum_bitcast_fusion
  883.7 44.3 %convolution_bitcast_fusion.2 = f32[2,2,256,128,64]{2,3,0,4,1:T(8,128)} fusion(f32[2,256,64,128,1]{3,2,1,0,4:T(8,128)} %maximum_bitcast_fusion, f32[1,128,128]{2,1,0:T(8,128)S(1)} %copy-done.6, f32[1,128,128]{2,1,0:T(8,128)S(1)} %copy-done.7), kind=kOutput, calls=%fused_computation.50 | convolution fusion | flops 12884934656 | bytes 50462720 | tf_op jit(solution)/shard_map/sbp,crap->scrba/dot_general | solution.py:55
  928.0 19.3 %slice_subtract_fusion = (f32[1,1,256,128,64]{2,3,0,4,1:T(8,128)}, f32[1,1,256,128,64]{2,3,0,4,1:T(8,128)}) fusion(f32[2,2,256,128,64]{2,3,0,4,1:T(8,128)} %convolution_bitcast_fusion.2), kind=kLoop, calls=%fused_computation.63 | loop fusion | flops 4194304 | bytes 50331648 | tf_op jit(solution)/shard_map/sub | solution.py:56
  947.3 8.4 copy.118
  955.7 8.3 copy.119
  963.9 4.8 pad_maximum_fusion
  968.7 6.4 copy.120
  975.1 4.6 all-to-all-start.3
  979.9 382.5 %all-to-all-done.3 = f32[2,256,32,256]{1,3,0,2:T(8,128)} async-done(((f32[2,256,32,256]{1,3,0,2:T(8,128)}), f32[2,256,32,256]{1,3,0,2:T(8,128)}, u32[]{:S(2)}, u32[]{:S(2)}) %all-to-all-start.3) | async-done | bytes 16777248 | tf_op jit(solution)/shard_map/all_to_all | solution.py:193
  1362.4 17.4 %copy.121 = f32[2,256,32,256]{3,1,2,0:T(8,128)} copy(f32[2,256,32,256]{1,3,0,2:T(8,128)} %all-to-all-done.3) | data formatting | bytes 33554432 | tf_op jit(solution)/shard_map/all_to_all | solution.py:193
  1379.8 44.0 %convolution_bitcast_fusion.1 = f32[2,2,64,128,256]{4,2,0,3,1:T(8,128)} fusion(f32[2,64,128,256,1]{3,2,1,0,4:T(8,128)} %bitcast.257, f32[1,64,64]{2,1,0:T(8,128)S(1)} %copy-done.2, f32[1,64,64]{2,1,0:T(8,128)S(1)} %copy-done.3), kind=kOutput, calls=%fused_computation.49 | convolution fusion | flops 6442459136 | bytes 50364416 | tf_op jit(solution)/shard_map/saq,cqpy->scapy/dot_general | solution.py:69
  1423.8 11.9 multiply_subtract_fusion
  1435.7 12.9 fusion.41
  1448.6 13.6 multiply_bitcast_fusion
  1462.2 8.1 copy.129
  1470.3 8.9 copy.130
  (398 shorter events, 203.9 us)
Async XLA Ops:
  1.4 9.8 all-to-all-start.1
  20.9 10.0 all-to-all-start.2
  249.0 31.9 %copy-start = (f32[16,32,72,2,64]{2,4,3,1,0:T(8,128)S(1)}, f32[16,32,72,2,64]{2,4,3,1,0:T(8,128)}, u32[]{:S(2)}) copy-start(f32[16,32,72,2,64]{2,4,3,1,0:T(8,128)} %get-tuple-element.158) | copy-start | bytes 56623108
  411.9 388.8 %collective-permute-start = (f32[2,8,8192]{2,1,0:T(8,128)}, f32[2,8,8192]{2,1,0:T(8,128)}, u32[]{:S(2)}, u32[]{:S(2)}) collective-permute-start(f32[2,8,8192]{2,1,0:T(8,128)} %reshape.664), channel_id=1, source_target_pairs={{0,1},{1,2},{2,3},{3,4},{4,5},{5,6},{6,7},{7,8},{8,9},{9,10},{10,1... | collective-permute-start | bytes 1572872 | tf_op jit(solution)/shard_map/ppermute | solution.py:19
  802.8 9.4 copy-start.2
  802.8 9.4 copy-start.3
  812.2 30.2 %copy-start.4 = (f32[64,128]{1,0:T(8,128)S(1)}, f32[64,128]{1,0:T(8,128)}, u32[]{:S(2)}) copy-start(f32[64,128]{1,0:T(8,128)} %get-tuple-element.199) | copy-start | bytes 98308
  812.3 30.2 %copy-start.5 = (f32[64,128]{1,0:T(8,128)S(1)}, f32[64,128]{1,0:T(8,128)}, u32[]{:S(2)}) copy-start(f32[64,128]{1,0:T(8,128)} %get-tuple-element.200) | copy-start | bytes 98308
  871.8 11.9 copy-start.6
  871.8 11.9 copy-start.7
  947.3 8.4 copy-start.1
  975.1 387.3 %all-to-all-start.3 = ((f32[2,256,32,256]{1,3,0,2:T(8,128)}), f32[2,256,32,256]{1,3,0,2:T(8,128)}, u32[]{:S(2)}, u32[]{:S(2)}) async-start(f32[2,256,32,256]{1,3,0,2:T(8,128)} %copy.120), calls=%async_computation.3 | async-start | bytes 33554432 | tf_op jit(solution)/shard_map/all_to_all | solution.py:193
where the time goes:
time: 1500 us; the launch traced here: 1480 us
  local copies, waits for them, and re-layouts  608 us (41%)
  waiting for transfers between devices  389 us (26%)
  matrix products  291 us (19%)
  other arithmetic  161 us (11%)
  starting transfers between devices  17.5 us (1%)
    all_to_all x1, waiting for transfers between devices, local(): lax.all_to_all(row_field.reshape(2, row_field.shape[1], device_count, col...  382 us
    scatter-add x1, local copies, waits for them, and re-layouts, grid_block(): tile_field.at[:, :, :, 1:, :kernel_width].add(beside_cols[:, :, :, :-1])  270 us
    unnamed x25, local copies, waits for them, and re-layouts  116 us
    dot_general x16, matrix products, patch_grid(): jnp.einsum('nako,to->nakt', selector, kernel, precision=highest)  69.8 us
    scatter-add x2, local copies, waits for them, and re-layouts, grid_block(): tile_field.at[:, 1:, :kernel_width, 1:, :kernel_width]  46.2 us
    dot_general x1, matrix products, row_transform(): jnp.einsum('sbp,crap->scrba', second_table, rotated, precision=highest)  44.3 us
    dot_general x1, matrix products, column_transform(): jnp.einsum('saq,cqpy->scapy', first_table, blocked, precision=highest)  44 us
    dot_general x16, matrix products, patch_grid(): jnp.einsum('nki,nckj->ncji', row_weights, scaled[..., PATCH:], precision=...  42.3 us
  transfers between devices with their start and end apart: 4, of which 3 were waited for; matrix products, arithmetic and copies ran while one was open for 26% of the time, Pallas kernels for 0%

commit v1 on v0

v1 whole, which is shorter than its diff:
```python
import math

import jax
import jax.numpy as jnp
from jax import lax
from jax.sharding import PartitionSpec as P

PATCH = 64
PR = 128
PC = 128


highest = lax.Precision.HIGH


def passed_along(value, axis, steps):
    count = lax.axis_size(axis)
    initial, last = (max(0, -steps), min(count, count - steps))
    return lax.ppermute(value, axis, [(source, source + steps) for source in range(initial, last)])


def fourier(length):
    index_list = jnp.arange(length, dtype=jnp.int32)
    angles = (
        2.0
        * math.pi
        / length
        * (index_list[:, None] * index_list[None, :] % length).astype(jnp.float32)
    )
    return jnp.stack([jnp.cos(angles), jnp.sin(angles)])


def twiddle(outer_size, inner_size, length):
    row_index = jnp.arange(outer_size, dtype=jnp.int32)[:, None]
    col_index = jnp.arange(inner_size, dtype=jnp.int32)[None, :]
    angles = 2.0 * math.pi / length * (row_index * col_index % length).astype(jnp.float32)
    return (jnp.cos(angles), jnp.sin(angles))


def complex_table(length):
    cos, sin = fourier(length)
    return jnp.stack([jnp.stack([cos, -sin]), jnp.stack([sin, cos])])


def row_transform(field):
    band_count, outer_size, _, rows, inner_size = field.shape
    length = outer_size * inner_size
    turn_cos, turn_sin = twiddle(outer_size, inner_size, length)
    product = jnp.einsum(
        "scaq,bqcip->sbiap", complex_table(outer_size), field, precision=highest
    )
    rotated = jnp.stack(
        [
            product[0] * turn_cos - product[1] * turn_sin,
            product[0] * turn_sin + product[1] * turn_cos,
        ]
    )
    result = jnp.einsum(
        "scyp,cbiap->sbiya", complex_table(inner_size), rotated, precision=highest
    )
    return result.reshape(2, band_count * rows, length)


def column_transform(received, image_scale):
    length = received.shape[1]
    item_count = received.shape[3]
    inner_size = 128
    outer_size = length // inner_size
    turn_cos, turn_sin = twiddle(outer_size, inner_size, length)
    blocked = received.reshape(2, outer_size, inner_size, item_count)
    product = jnp.einsum(
        "scaq,cqpy->sapy", complex_table(outer_size), blocked, precision=highest
    )
    turn_cos = turn_cos[..., None]
    turn_sin = turn_sin[..., None]
    rotated = jnp.stack(
        [
            product[0] * turn_cos - product[1] * turn_sin,
            product[0] * turn_sin + product[1] * turn_cos,
        ]
    )
    last_table = complex_table(inner_size)[0] * image_scale
    image_rows = jnp.einsum("cbp,capy->yba", last_table, rotated, precision=highest)
    return image_rows.reshape(item_count, length)


def joined(array, group):
    count, lead, slots = array.shape
    blocks = array.reshape(count // group, group, lead, slots)
    before = jnp.roll(blocks[:, group - 1], 1, axis=0)
    return jnp.concatenate([before] + [blocks[:, step] for step in range(group)], axis=-1)


def spread(distance, taps):
    weights = jnp.zeros(distance.shape, jnp.float32)
    for tap_step in range(taps.shape[1]):
        weights = jnp.where(distance == tap_step, taps[:, tap_step][:, None], weights)
    return weights


def band_tiles(values, positions, counts, kernel):
    kernel_width, oversample = kernel.shape
    column_count, _, slot_count = values.shape
    width = 128
    group = width // PATCH
    group_count = column_count // group
    live_mask = jnp.arange(slot_count, dtype=jnp.int32)[None, :] < counts[:, None]
    cell_index = positions // oversample
    fine_index = positions - cell_index * oversample
    selector = (
        fine_index[:, :, None, :] == jnp.arange(oversample, dtype=jnp.int32)[:, None]
    ).astype(jnp.float32)
    taps = jnp.einsum("to,naok->natk", kernel, selector, precision=highest)
    taps = joined(taps.reshape(column_count, 2 * kernel_width, slot_count), group)
    cells = joined(cell_index, group)
    scaled = joined(jnp.where(live_mask[:, None], values, 0.0), group)
    extent = PATCH + kernel_width
    row_distance = (
        jnp.arange(extent, dtype=jnp.int32)[None, :, None] - (cells[:, 0] % PATCH)[:, None]
    )
    starts = jnp.arange(group_count, dtype=jnp.int32) * width
    columns = starts[:, None] + jnp.arange(width, dtype=jnp.int32)
    column_distance = columns[:, :, None] - cells[:, 1][:, None]
    row_weights = spread(row_distance, taps[:, :kernel_width])
    column_weights = spread(column_distance, taps[:, kernel_width:])
    scaled_rows = scaled[:, :, None] * row_weights[:, None]
    return jnp.einsum("mcik,mjk->mcij", scaled_rows, column_weights, precision=highest)


def local(vis_value, vis_pos, counts, kernel):
    kernel_width = kernel.shape[0]
    device_count = lax.axis_size("au") * lax.axis_size("vert")
    slot_count = vis_value.shape[3]
    image_scale = 1.0 / math.sqrt(PR * PC * slot_count)
    vert_count = lax.axis_size("vert")
    band_count = vis_value.shape[0] // vert_count
    local_columns = vis_value.shape[1]
    moved_values = lax.all_to_all(
        vis_value.reshape(vert_count, band_count, local_columns, 2, slot_count),
        "vert",
        split_axis=0,
        concat_axis=2,
        tiled=True,
    )
    positions, tallies = (
        lax.all_to_all(
            vis_pos.reshape(vert_count, band_count, local_columns, 2, slot_count),
            "vert",
            split_axis=0,
            concat_axis=2,
            tiled=True,
        ),
        lax.all_to_all(
            counts.reshape(vert_count, band_count, local_columns),
            "vert",
            split_axis=0,
            concat_axis=2,
            tiled=True,
        ),
    )
    column_count = local_columns * vert_count
    values = moved_values.reshape(band_count, column_count, 2, slot_count)
    positions = positions.reshape(band_count, column_count, 2, slot_count)
    tallies = tallies.reshape(band_count, column_count)
    tiles = lax.map(lambda members: band_tiles(*members, kernel), (values, positions, tallies))
    spill = tiles[..., PATCH:, :]
    arrived = passed_along(spill[-1], ("au", "vert"), 1)
    above = jnp.concatenate([arrived[None], spill[:-1]], axis=0)
    field = jnp.concatenate(
        [tiles[..., :kernel_width, :] + above, tiles[..., kernel_width:PATCH, :]], axis=3
    )
    row_field = row_transform(field)
    length = row_field.shape[2]
    column_share = length // device_count
    return column_transform(
        lax.all_to_all(
            row_field.reshape(2, row_field.shape[1], device_count, column_share),
            ("au", "vert"),
            split_axis=2,
            concat_axis=1,
            tiled=True,
        ),
        image_scale,
    )


def solution(mesh):
    in_specs = (P("au", "vert", None, None), P("au", "vert", None, None), P("au", "vert"), P())
    out_specs = P(("au", "vert"), None)
    return jax.shard_map(local, mesh=mesh, in_specs=in_specs, out_specs=out_specs, check_vma=False)
```

time: 1500 us -> 796 us (0.53)
  local copies, waits for them, and re-layouts: 608 us -> 145 us
  matrix products: 291 us -> 160 us
  other arithmetic: 161 us -> 63.3 us
    scatter-add x4 -> x0, local copies, waits for them, and re-layouts: 325 us -> none  [the longest x1 270 us: grid_block(): tile_field.at[:, :, :, 1:, :kernel_width].add(beside_cols[:, :, :, :-1])]
    unnamed x25 -> x12, local copies, waits for them, and re-layouts: 116 us -> 5.28 us
    dot_general x37 -> x12, matrix products: 257 us -> 160 us  [the longest x4 74.2 us: band_tiles(): jnp.einsum('mcik,mjk->mcij', scaled_rows, column_weights, precision=highest)]
    add x19 -> x5, other arithmetic: 69.9 us -> 2.27 us  [the longest x1 1.98 us: local(): tiles[..., :kernel_width, :] + above]
    sub x3 -> x10, other arithmetic: 60.5 us -> 24.1 us  [the longest x1 13.8 us: column_transform(): product[0] * turn_cos - product[1] * turn_sin]
    transpose x0 -> x2, local copies, waits for them, and re-layouts: none -> 34.5 us  [the longest x1 23 us: row_transform(): jnp.einsum('scyp,cbiap->sbiya', complex_table(inner_size), rotated, preci...]
    while x16 -> x0, matrix products: 34.3 us -> none
    reshape x3 -> x2, local copies, waits for them, and re-layouts: 39.2 us -> 8.98 us  [the longest x1 8.89 us: column_transform(): return image_rows.reshape(item_count, length)]
  transfers between devices with their start and end apart: 4 -> 5, of which waited for: 3 -> 4; matrix products, arithmetic and copies ran while one was open for 26% -> 3% of each run, Pallas kernels for 0% -> 0%
where the time goes in v1:
time: 796 us; the launch traced here: 784 us
  waiting for transfers between devices  394 us (49%)
  matrix products  160 us (20%)
  local copies, waits for them, and re-layouts  145 us (18%)
  other arithmetic  63.3 us (8%)
  starting transfers between devices  20.7 us (3%)
    all_to_all x1, waiting for transfers between devices, local(): lax.all_to_all(row_field.reshape(2, row_field.shape[1], device_count, col...  382 us
    dot_general x4, matrix products, band_tiles(): jnp.einsum('mcik,mjk->mcij', scaled_rows, column_weights, precision=highest)  74.2 us
    another operation x2, local copies, waits for them, and re-layouts, local(): row_field.reshape(2, row_field.shape[1], device_count, column_share)  43.8 us
    dot_general x1, matrix products, column_transform(): jnp.einsum('scaq,cqpy->sapy', complex_table(outer_size), blocked, precisi...  25.6 us
    select_n x4, other arithmetic, spread(): jnp.where(distance == tap_step, taps[:, tap_step][:, None], weights)  24.8 us
    transpose x1, local copies, waits for them, and re-layouts, row_transform(): jnp.einsum('scyp,cbiap->sbiya', complex_table(inner_size), rotated, preci...  23 us
    dot_general x4, matrix products, band_tiles(): taps = jnp.einsum('to,naok->natk', kernel, selector, precision=highest)  19.3 us
  transfers between devices with their start and end apart: 5, of which 4 were waited for; matrix products, arithmetic and copies ran while one was open for 3% of the time, Pallas kernels for 0%

profile of v1, /device:TPU:0, one launch (start us, length us, event | category | flops | bytes accessed | tf_op | source)
XLA Modules:
  0.0 784.5 jit_solution(12170232325561670538)
XLA Ops:
  1.4 5.2 all-to-all-start
  6.5 1.9 copy.110
  8.4 2.8 all-to-all-done
  11.2 3.5 all-to-all-start.1
  14.7 1.9 copy.112
  16.6 4.8 all-to-all-done.1
  21.4 3.5 all-to-all-start.2
  27.8 3.6 all-to-all-done.2
  31.5 147.3 %while.12 = (s32[]{:T(128)}, f32[4,64,2,72,128]{4,1,2,3,0:T(8,128)}, s32[4,128]{1,0:T(4,128)S(1)}, f32[4,128,2,128]{3,1,2,0:T(8,128)S(1)}, s32[4,128,2,128]{3,1,2,0:T(8,128)S(1)}, /*index=5*/f32[8,128]{1,0:T(8,128)}, s32[]{:T(128)}) while((s32[]{:T(128)}, f32[4,64,2,72,128]{4,1,2,3,0:T(8,128)}, s32[4,128]{1,0:T(4,128)S(1)}, ...), condition=%wide.region_1.2_spmd, body=%wide.region_0.1_spmd.sunk | while | flops 3013378048 | bytes 48205400 | solution.py:165
  31.7 4.8 fusion.141
  36.8 1.4 fusion.142
  38.9 6.2 select_select_fusion.2
  46.1 18.5 %fusion.147 = f32[1,64,2,72,128]{4,3,2,1,0:T(8,128)S(1)} fusion(f32[64,384]{1,0:T(8,128)S(1)} %get-tuple-element.238, f32[64,384]{1,0:T(8,128)S(1)} %get-tuple-element.239, f32[64,384]{1,0:T(8,128)S(1)} %get-tuple-element.242, f32[64,384]{1,0:T(8,128)S(1)} %get-tuple-element.243, f32[64,384]{1,0:T(8,128)S(1)} %get-tuple-element.246, ...), kind=kOutput, calls=%fused_computation.54.clone.1 | convolution fusion | flops 2774925312 | bytes 12910592 | tf_op jit(solution)/shard_map/while/body/eval_jaxpr/mcik,mjk->mcij/dot_general | solution.py:127
  64.7 3.6 copy_dynamic-update-slice_fusion.2
  68.4 4.8 fusion.141
  73.5 1.4 fusion.142
  75.6 6.2 select_select_fusion.2
  82.8 18.5 %fusion.147 = f32[1,64,2,72,128]{4,3,2,1,0:T(8,128)S(1)} fusion(f32[64,384]{1,0:T(8,128)S(1)} %get-tuple-element.238, f32[64,384]{1,0:T(8,128)S(1)} %get-tuple-element.239, f32[64,384]{1,0:T(8,128)S(1)} %get-tuple-element.242, f32[64,384]{1,0:T(8,128)S(1)} %get-tuple-element.243, f32[64,384]{1,0:T(8,128)S(1)} %get-tuple-element.246, ...), kind=kOutput, calls=%fused_computation.54.clone.1 | convolution fusion | flops 2774925312 | bytes 12910592 | tf_op jit(solution)/shard_map/while/body/eval_jaxpr/mcik,mjk->mcij/dot_general | solution.py:127
  101.4 3.6 copy_dynamic-update-slice_fusion.2
  105.2 4.8 fusion.141
  110.3 1.4 fusion.142
  112.3 6.2 select_select_fusion.2
  119.6 18.5 %fusion.147 = f32[1,64,2,72,128]{4,3,2,1,0:T(8,128)S(1)} fusion(f32[64,384]{1,0:T(8,128)S(1)} %get-tuple-element.238, f32[64,384]{1,0:T(8,128)S(1)} %get-tuple-element.239, f32[64,384]{1,0:T(8,128)S(1)} %get-tuple-element.242, f32[64,384]{1,0:T(8,128)S(1)} %get-tuple-element.243, f32[64,384]{1,0:T(8,128)S(1)} %get-tuple-element.246, ...), kind=kOutput, calls=%fused_computation.54.clone.1 | convolution fusion | flops 2774925312 | bytes 12910592 | tf_op jit(solution)/shard_map/while/body/eval_jaxpr/mcik,mjk->mcij/dot_general | solution.py:127
  138.1 3.7 copy_dynamic-update-slice_fusion.2
  142.0 4.8 fusion.141
  147.1 1.4 fusion.142
  149.1 6.2 select_select_fusion.2
  156.3 18.5 %fusion.147 = f32[1,64,2,72,128]{4,3,2,1,0:T(8,128)S(1)} fusion(f32[64,384]{1,0:T(8,128)S(1)} %get-tuple-element.238, f32[64,384]{1,0:T(8,128)S(1)} %get-tuple-element.239, f32[64,384]{1,0:T(8,128)S(1)} %get-tuple-element.242, f32[64,384]{1,0:T(8,128)S(1)} %get-tuple-element.243, f32[64,384]{1,0:T(8,128)S(1)} %get-tuple-element.246, ...), kind=kOutput, calls=%fused_computation.54.clone.1 | convolution fusion | flops 2774925312 | bytes 12910592 | tf_op jit(solution)/shard_map/while/body/eval_jaxpr/mcik,mjk->mcij/dot_general | solution.py:127
  174.9 3.6 copy_dynamic-update-slice_fusion.2
  179.9 3.4 collective-permute-start
  184.0 1.5 slice.264
  185.6 13.6 %slice.265 = f32[4,64,2,56,128]{4,1,2,3,0:T(8,128)} slice(f32[4,64,2,72,128]{4,1,2,3,0:T(8,128)} %get-tuple-element.85), slice={[0:4], [0:64], [0:2], [8:64], [0:128]} | slice | bytes 29360128 | tf_op jit(solution)/shard_map/slice | solution.py:170
  199.1 2.0 maximum_add_fusion
  201.1 13.5 %fusion.77 = f32[2,4,64,64,128]{4,3,0,2,1:T(8,128)} fusion(f32[4,64,2,56,128]{4,1,2,3,0:T(8,128)} %slice.265, f32[4,64,2,8,128]{4,1,2,3,0:T(8,128)S(1)} %maximum_add_fusion, f32[1,2,64,64]{3,2,1,0:T(8,128)S(1)} %get-tuple-element.147, f32[1,2,64,64]{3,2,1,0:T(8,128)S(1)} %get-tuple-element.146), kind=kOutput, calls=%fused_computation.136 | convolution fusion | flops 3225436160 | bytes 33619968 | tf_op jit(solution)/shard_map/scaq,bqcip->sbiap/dot_general | solution.py:49
  214.6 9.8 %multiply_subtract_fusion.1 = (f32[1,4,64,64,128]{4,3,0,2,1:T(8,128)S(1)}, f32[1,4,64,64,128]{4,3,0,2,1:T(8,128)}) fusion(f32[2,4,64,64,128]{4,3,0,2,1:T(8,128)} %fusion.77, f32[64,128]{1,0:T(8,128)S(1)} %copy-done, f32[64,128]{1,0:T(8,128)S(1)} %copy-done.1), kind=kLoop, calls=%fused_computation.140 | loop fusion | flops 12582912 | bytes 33619968 | tf_op jit(solution)/shard_map/sub | solution.py:54
  224.4 12.7 %fusion.76 = f32[2,4,64,128,64]{3,4,0,2,1:T(8,128)} fusion(f32[1,4,64,64,128]{4,3,0,2,1:T(8,128)} %get-tuple-element.143, f32[1,4,64,64,128]{4,3,0,2,1:T(8,128)S(1)} %get-tuple-element.142, f32[1,2,128,128]{3,2,1,0:T(8,128)S(1)} %get-tuple-element.145, f32[1,2,128,128]{3,2,1,0:T(8,128)S(1)} %get-tuple-element.144), kind=kOutput, calls=%fused_computation.135 | convolution fusion | flops 6446710784 | bytes 33816576 | tf_op jit(solution)/shard_map/scyp,cbiap->sbiya/dot_general | solution.py:58
  237.1 23.0 %copy.118 = f32[2,4,64,128,64]{4,3,2,1,0:T(8,128)} copy(f32[2,4,64,128,64]{3,4,0,2,1:T(8,128)} %fusion.76) | data formatting | bytes 33554432 | tf_op jit(solution)/shard_map/scyp,cbiap->sbiya/transpose | solution.py:58
  260.1 27.9 %reshape_reshape.3 = f32[2,256,32,256]{3,2,1,0:T(8,128)} reshape(f32[2,4,64,128,64]{4,3,2,1,0:T(8,128)} %copy.118) | data formatting | bytes 33554432 | tf_op jit(solution)/shard_map/reshape;reshape | solution.py:177
  288.0 15.9 %copy.119 = f32[2,256,32,256]{3,1,0,2:T(8,128)} copy(f32[2,256,32,256]{3,2,1,0:T(8,128)} %reshape_reshape.3) | data formatting | bytes 33554432 | tf_op jit(solution)/shard_map/reshape;reshape | solution.py:177
  303.9 5.2 all-to-all-start.3
  309.3 382.5 %all-to-all-done.3 = f32[2,256,32,256]{3,1,0,2:T(8,128)} async-done(((f32[2,256,32,256]{3,1,0,2:T(8,128)}), f32[2,256,32,256]{3,1,0,2:T(8,128)}, u32[]{:S(2)}, u32[]{:S(2)}) %all-to-all-start.3) | async-done | bytes 16777248 | tf_op jit(solution)/shard_map/all_to_all | solution.py:176
  691.8 11.5 %copy.120 = f32[2,256,32,256]{3,1,2,0:T(8,128)} copy(f32[2,256,32,256]{3,1,0,2:T(8,128)} %all-to-all-done.3) | data formatting | bytes 33554432 | tf_op jit(solution)/shard_map/all_to_all | solution.py:176
  703.3 25.6 %fusion.78 = f32[2,64,128,256]{3,1,2,0:T(8,128)} fusion(f32[2,64,128,256]{3,2,1,0:T(8,128)} %bitcast.254, f32[1,2,64,64]{3,2,1,0:T(8,128)S(1)} %get-tuple-element.147, f32[1,2,64,64]{3,2,1,0:T(8,128)S(1)} %get-tuple-element.146), kind=kOutput, calls=%fused_computation.141 | convolution fusion | flops 3221241856 | bytes 33619968 | tf_op jit(solution)/shard_map/scaq,cqpy->sapy/dot_general | solution.py:71
  728.9 13.8 %multiply_subtract_fusion = (f32[1,64,128,256]{3,1,2,0:T(8,128)}, f32[1,64,128,256]{3,1,2,0:T(8,128)}) fusion(f32[2,64,128,256]{3,1,2,0:T(8,128)} %fusion.78, f32[64,128]{0,1:T(8,128)S(1)} %copy.123, f32[64,128]{0,1:T(8,128)S(1)} %copy.122), kind=kLoop, calls=%fused_computation.138 | loop fusion | flops 12582912 | bytes 33619968 | tf_op jit(solution)/shard_map/sub | solution.py:78
  742.7 6.5 pad_maximum_fusion.2
  749.2 14.5 %fusion.81 = f32[256,128,64]{0,1,2:T(8,128)} fusion(f32[2,64,128,256]{3,1,2,0:T(8,128)S(1)} %pad_maximum_fusion.2, f32[1,128,128]{2,1,0:T(8,128)S(1)} %fusion.112, f32[1,128,128]{2,1,0:T(8,128)S(1)} %get-tuple-element.153), kind=kOutput, calls=%fused_computation.142 | convolution fusion | flops 3221291008 | bytes 25296896 | tf_op jit(solution)/shard_map/cbp,capy->yba/dot_general | solution.py:83
  763.7 11.5 %copy.125 = f32[256,128,64]{0,2,1:T(8,128)} copy(f32[256,128,64]{0,1,2:T(8,128)} %fusion.81) | data formatting | bytes 16777216 | tf_op jit(solution)/shard_map/cbp,capy->yba/transpose | solution.py:83
  775.2 8.9 %copy.126 = f32[256,8192]{1,0:T(8,128)} copy(f32[256,8192]{0,1:T(8,128)} %bitcast.258) | data formatting | bytes 16777216 | tf_op jit(solution)/shard_map/reshape | solution.py:84
  (164 shorter events, 13.9 us)
Async XLA Ops:
  1.4 9.9 %all-to-all-start = ((s32[4,1,128]{2,1,0:T(1,128)}), s32[4,1,128]{2,1,0:T(1,128)S(1)}, u32[]{:S(2)}, u32[]{:S(2)}) async-start(s32[4,1,128]{2,1,0:T(1,128)} %reshape.440), calls=%async_computation | async-start | bytes 4096 | tf_op jit(solution)/shard_map/all_to_all | solution.py:153
  11.2 10.2 %all-to-all-start.1 = ((f32[4,4,32,2,128]{4,2,3,1,0:T(8,128)}), f32[4,4,32,2,128]{4,2,3,1,0:T(8,128)S(1)}, u32[]{:S(2)}, u32[]{:S(2)}) async-start(f32[4,4,32,2,128]{4,2,3,1,0:T(8,128)} %bitcast.32), calls=%async_computation.1 | async-start | bytes 1048576 | tf_op jit(solution)/shard_map/all_to_all | solution.py:138
  21.4 10.0 %all-to-all-start.2 = ((s32[4,4,32,2,128]{4,2,3,1,0:T(8,128)}), s32[4,4,32,2,128]{4,2,3,1,0:T(8,128)S(1)}, u32[]{:S(2)}, u32[]{:S(2)}) async-start(s32[4,4,32,2,128]{4,2,3,1,0:T(8,128)} %bitcast.36), calls=%async_computation.2 | async-start | bytes 1048576 | tf_op jit(solution)/shard_map/all_to_all | solution.py:146
  31.5 152.5 %copy-start.2 = (f32[1,64,64]{2,1,0:T(8,128)S(1)}, f32[1,64,64]{2,1,0:T(8,128)}, u32[]{:S(2)}) copy-start(f32[1,64,64]{2,1,0:T(8,128)} %get-tuple-element.148) | copy-start | bytes 49156
  31.5 152.5 %copy-start.3 = (f32[1,64,64]{2,1,0:T(8,128)S(1)}, f32[1,64,64]{2,1,0:T(8,128)}, u32[]{:S(2)}) copy-start(f32[1,64,64]{2,1,0:T(8,128)} %get-tuple-element.149) | copy-start | bytes 49156
  179.9 19.3 %collective-permute-start = (f32[64,2,8,128]{3,0,1,2:T(8,128)S(1)}, f32[64,2,8,128]{3,0,1,2:T(8,128)S(1)}, u32[]{:S(2)}, u32[]{:S(2)}) collective-permute-start(f32[64,2,8,128]{3,0,1,2:T(8,128)S(1)} %slice_bitcast_fusion.7), channel_id=1, source_target_pairs={{0,1},{1,2},{2,3},{3,4},{4,5},{5,6},{6,7},{7,8},{8,9},{9,10},{10,1... | collective-permute-start | bytes 1572872 | tf_op jit(solution)/shard_map/ppermute | solution.py:19
  201.1 13.5 %copy-start = (f32[64,128]{1,0:T(8,128)S(1)}, f32[64,128]{1,0:T(8,128)}, u32[]{:S(2)}) copy-start(f32[64,128]{1,0:T(8,128)} %get-tuple-element.150) | copy-start | bytes 98308
  201.1 13.5 %copy-start.1 = (f32[64,128]{1,0:T(8,128)S(1)}, f32[64,128]{1,0:T(8,128)}, u32[]{:S(2)}) copy-start(f32[64,128]{1,0:T(8,128)} %get-tuple-element.151) | copy-start | bytes 98308
  303.9 387.9 %all-to-all-start.3 = ((f32[2,256,32,256]{3,1,0,2:T(8,128)}), f32[2,256,32,256]{3,1,0,2:T(8,128)}, u32[]{:S(2)}, u32[]{:S(2)}) async-start(f32[2,256,32,256]{3,1,0,2:T(8,128)} %copy.119), calls=%async_computation.3 | async-start | bytes 33554432 | tf_op jit(solution)/shard_map/all_to_all | solution.py:176

commit v2 on v1

--- a/solution.py
+++ b/solution.py
@@ -64,7 +64,7 @@
 def column_transform(received, image_scale):
     length = received.shape[1]
     item_count = received.shape[3]
-    inner_size = 128
+    inner_size = length // 128
     outer_size = length // inner_size
     turn_cos, turn_sin = twiddle(outer_size, inner_size, length)
     blocked = received.reshape(2, outer_size, inner_size, item_count)

time: 796 us -> 791 us (level)
  no operation moved by 1% of the time
where the time goes in v2:
time: 791 us; the launch traced here: 779 us
  waiting for transfers between devices  394 us (50%)
  matrix products  160 us (20%)
  local copies, waits for them, and re-layouts  145 us (18%)
  other arithmetic  57.6 us (7%)
  starting transfers between devices  20.7 us (3%)
    all_to_all x1, waiting for transfers between devices, local(): lax.all_to_all(row_field.reshape(2, row_field.shape[1], device_count, col...  383 us
    dot_general x4, matrix products, band_tiles(): jnp.einsum('mcik,mjk->mcij', scaled_rows, column_weights, precision=highest)  74.2 us
    another operation x2, local copies, waits for them, and re-layouts, local(): row_field.reshape(2, row_field.shape[1], device_count, column_share)  43.8 us
    dot_general x1, matrix products, column_transform(): jnp.einsum('scaq,cqpy->sapy', complex_table(outer_size), blocked, precisi...  25.9 us
    select_n x4, other arithmetic, spread(): jnp.where(distance == tap_step, taps[:, tap_step][:, None], weights)  24.8 us
    transpose x1, local copies, waits for them, and re-layouts, row_transform(): jnp.einsum('scyp,cbiap->sbiya', complex_table(inner_size), rotated, preci...  23 us
    dot_general x4, matrix products, band_tiles(): taps = jnp.einsum('to,naok->natk', kernel, selector, precision=highest)  19.3 us
  transfers between devices with their start and end apart: 5, of which 4 were waited for; matrix products, arithmetic and copies ran while one was open for 3% of the time, Pallas kernels for 0%

profile of v2, /device:TPU:0, one launch (start us, length us, event | category | flops | bytes accessed | tf_op | source)
XLA Modules:
  0.0 779.1 jit_solution(10357679683218870775)
XLA Ops:
  1.4 5.2 all-to-all-start
  6.5 1.9 copy.102
  8.4 2.6 all-to-all-done
  11.1 3.5 all-to-all-start.1
  14.6 1.9 copy.104
  16.5 5.1 all-to-all-done.1
  21.5 3.5 all-to-all-start.2
  28.0 3.6 all-to-all-done.2
  31.6 147.3 %while.12 = (s32[]{:T(128)}, f32[4,64,2,72,128]{4,1,2,3,0:T(8,128)}, s32[4,128]{1,0:T(4,128)S(1)}, f32[4,128,2,128]{3,1,2,0:T(8,128)S(1)}, s32[4,128,2,128]{3,1,2,0:T(8,128)S(1)}, /*index=5*/f32[8,128]{1,0:T(8,128)}, s32[]{:T(128)}) while((s32[]{:T(128)}, f32[4,64,2,72,128]{4,1,2,3,0:T(8,128)}, s32[4,128]{1,0:T(4,128)S(1)}, ...), condition=%wide.region_1.2_spmd, body=%wide.region_0.1_spmd.sunk | while | flops 3013378048 | bytes 48205400 | solution.py:165
  31.8 4.8 fusion.149
  36.9 1.4 fusion.150
  39.0 6.2 select_select_fusion.2
  46.2 18.5 %fusion.155 = f32[1,64,2,72,128]{4,3,2,1,0:T(8,128)S(1)} fusion(f32[64,384]{1,0:T(8,128)S(1)} %get-tuple-element.240, f32[64,384]{1,0:T(8,128)S(1)} %get-tuple-element.241, f32[64,384]{1,0:T(8,128)S(1)} %get-tuple-element.244, f32[64,384]{1,0:T(8,128)S(1)} %get-tuple-element.245, f32[64,384]{1,0:T(8,128)S(1)} %get-tuple-element.248, ...), kind=kOutput, calls=%fused_computation.54.clone.1 | convolution fusion | flops 2774925312 | bytes 12910592 | tf_op jit(solution)/shard_map/while/body/eval_jaxpr/mcik,mjk->mcij/dot_general | solution.py:127
  64.8 3.6 copy_dynamic-update-slice_fusion.2
  68.6 4.8 fusion.149
  73.6 1.4 fusion.150
  75.7 6.2 select_select_fusion.2
  82.9 18.5 %fusion.155 = f32[1,64,2,72,128]{4,3,2,1,0:T(8,128)S(1)} fusion(f32[64,384]{1,0:T(8,128)S(1)} %get-tuple-element.240, f32[64,384]{1,0:T(8,128)S(1)} %get-tuple-element.241, f32[64,384]{1,0:T(8,128)S(1)} %get-tuple-element.244, f32[64,384]{1,0:T(8,128)S(1)} %get-tuple-element.245, f32[64,384]{1,0:T(8,128)S(1)} %get-tuple-element.248, ...), kind=kOutput, calls=%fused_computation.54.clone.1 | convolution fusion | flops 2774925312 | bytes 12910592 | tf_op jit(solution)/shard_map/while/body/eval_jaxpr/mcik,mjk->mcij/dot_general | solution.py:127
  101.5 3.6 copy_dynamic-update-slice_fusion.2
  105.3 4.8 fusion.149
  110.4 1.4 fusion.150
  112.5 6.2 select_select_fusion.2
  119.7 18.5 %fusion.155 = f32[1,64,2,72,128]{4,3,2,1,0:T(8,128)S(1)} fusion(f32[64,384]{1,0:T(8,128)S(1)} %get-tuple-element.240, f32[64,384]{1,0:T(8,128)S(1)} %get-tuple-element.241, f32[64,384]{1,0:T(8,128)S(1)} %get-tuple-element.244, f32[64,384]{1,0:T(8,128)S(1)} %get-tuple-element.245, f32[64,384]{1,0:T(8,128)S(1)} %get-tuple-element.248, ...), kind=kOutput, calls=%fused_computation.54.clone.1 | convolution fusion | flops 2774925312 | bytes 12910592 | tf_op jit(solution)/shard_map/while/body/eval_jaxpr/mcik,mjk->mcij/dot_general | solution.py:127
  138.2 3.7 copy_dynamic-update-slice_fusion.2
  142.1 4.8 fusion.149
  147.2 1.4 fusion.150
  149.3 6.2 select_select_fusion.2
  156.5 18.5 %fusion.155 = f32[1,64,2,72,128]{4,3,2,1,0:T(8,128)S(1)} fusion(f32[64,384]{1,0:T(8,128)S(1)} %get-tuple-element.240, f32[64,384]{1,0:T(8,128)S(1)} %get-tuple-element.241, f32[64,384]{1,0:T(8,128)S(1)} %get-tuple-element.244, f32[64,384]{1,0:T(8,128)S(1)} %get-tuple-element.245, f32[64,384]{1,0:T(8,128)S(1)} %get-tuple-element.248, ...), kind=kOutput, calls=%fused_computation.54.clone.1 | convolution fusion | flops 2774925312 | bytes 12910592 | tf_op jit(solution)/shard_map/while/body/eval_jaxpr/mcik,mjk->mcij/dot_general | solution.py:127
  175.0 3.6 copy_dynamic-update-slice_fusion.2
  180.0 3.4 collective-permute-start
  184.2 1.5 slice.264
  185.7 13.6 %slice.265 = f32[4,64,2,56,128]{4,1,2,3,0:T(8,128)} slice(f32[4,64,2,72,128]{4,1,2,3,0:T(8,128)} %get-tuple-element.85), slice={[0:4], [0:64], [0:2], [8:64], [0:128]} | slice | bytes 29360128 | tf_op jit(solution)/shard_map/slice | solution.py:170
  199.3 2.0 maximum_add_fusion
  201.3 13.5 %fusion.77 = f32[2,4,64,64,128]{4,3,0,2,1:T(8,128)} fusion(f32[4,64,2,56,128]{4,1,2,3,0:T(8,128)} %slice.265, f32[4,64,2,8,128]{4,1,2,3,0:T(8,128)S(1)} %maximum_add_fusion, f32[1,2,64,64]{3,2,1,0:T(8,128)S(1)} %get-tuple-element.147, f32[1,2,64,64]{3,2,1,0:T(8,128)S(1)} %get-tuple-element.146), kind=kOutput, calls=%fused_computation.136 | convolution fusion | flops 3225436160 | bytes 33619968 | tf_op jit(solution)/shard_map/scaq,bqcip->sbiap/dot_general | solution.py:49
  214.8 9.8 %multiply_subtract_fusion.1 = (f32[1,4,64,64,128]{4,3,0,2,1:T(8,128)S(1)}, f32[1,4,64,64,128]{4,3,0,2,1:T(8,128)}) fusion(f32[2,4,64,64,128]{4,3,0,2,1:T(8,128)} %fusion.77, f32[64,128]{1,0:T(8,128)S(1)} %copy-done.2, f32[64,128]{1,0:T(8,128)S(1)} %copy-done.3), kind=kLoop, calls=%fused_computation.140 | loop fusion | flops 12582912 | bytes 33619968 | tf_op jit(solution)/shard_map/sub | solution.py:54
  224.6 12.7 %fusion.76 = f32[2,4,64,128,64]{3,4,0,2,1:T(8,128)} fusion(f32[1,4,64,64,128]{4,3,0,2,1:T(8,128)} %get-tuple-element.143, f32[1,4,64,64,128]{4,3,0,2,1:T(8,128)S(1)} %get-tuple-element.142, f32[1,2,128,128]{3,2,1,0:T(8,128)S(1)} %get-tuple-element.145, f32[1,2,128,128]{3,2,1,0:T(8,128)S(1)} %get-tuple-element.144), kind=kOutput, calls=%fused_computation.135 | convolution fusion | flops 6446710784 | bytes 33816576 | tf_op jit(solution)/shard_map/scyp,cbiap->sbiya/dot_general | solution.py:58
  237.2 23.0 %copy.110 = f32[2,4,64,128,64]{4,3,2,1,0:T(8,128)} copy(f32[2,4,64,128,64]{3,4,0,2,1:T(8,128)} %fusion.76) | data formatting | bytes 33554432 | tf_op jit(solution)/shard_map/scyp,cbiap->sbiya/transpose | solution.py:58
  260.3 27.9 %reshape_reshape.3 = f32[2,256,32,256]{3,2,1,0:T(8,128)} reshape(f32[2,4,64,128,64]{4,3,2,1,0:T(8,128)} %copy.110) | data formatting | bytes 33554432 | tf_op jit(solution)/shard_map/reshape;reshape | solution.py:177
  288.2 15.9 %copy.111 = f32[2,256,32,256]{3,1,0,2:T(8,128)} copy(f32[2,256,32,256]{3,2,1,0:T(8,128)} %reshape_reshape.3) | data formatting | bytes 33554432 | tf_op jit(solution)/shard_map/reshape;reshape | solution.py:177
  304.1 5.2 all-to-all-start.3
  309.4 382.5 %all-to-all-done.3 = f32[2,256,32,256]{3,1,0,2:T(8,128)} async-done(((f32[2,256,32,256]{3,1,0,2:T(8,128)}), f32[2,256,32,256]{3,1,0,2:T(8,128)}, u32[]{:S(2)}, u32[]{:S(2)}) %all-to-all-start.3) | async-done | bytes 16777248 | tf_op jit(solution)/shard_map/all_to_all | solution.py:176
  691.9 11.5 %copy.112 = f32[2,256,32,256]{3,1,2,0:T(8,128)} copy(f32[2,256,32,256]{3,1,0,2:T(8,128)} %all-to-all-done.3) | data formatting | bytes 33554432 | tf_op jit(solution)/shard_map/all_to_all | solution.py:176
  703.4 25.9 %fusion.78 = f32[2,128,64,256]{3,1,2,0:T(8,128)} fusion(f32[2,128,64,256]{3,2,1,0:T(8,128)} %bitcast.254, f32[1,2,128,128]{3,2,1,0:T(8,128)S(1)} %get-tuple-element.145, f32[1,2,128,128]{3,2,1,0:T(8,128)S(1)} %get-tuple-element.144), kind=kOutput, calls=%fused_computation.141 | convolution fusion | flops 6442516480 | bytes 33816576 | tf_op jit(solution)/shard_map/scaq,cqpy->sapy/dot_general | solution.py:71
  729.3 9.8 %multiply_subtract_fusion = (f32[1,128,64,256]{3,1,2,0:T(8,128)S(1)}, f32[1,128,64,256]{3,1,2,0:T(8,128)}) fusion(f32[2,128,64,256]{3,1,2,0:T(8,128)} %fusion.78, f32[128,64]{0,1:T(8,128)S(1)} %get-tuple-element.154, f32[128,64]{0,1:T(8,128)S(1)} %get-tuple-element.155), kind=kLoop, calls=%fused_computation.138 | loop fusion | flops 12582912 | bytes 33619968 | tf_op jit(solution)/shard_map/sub | solution.py:78
  739.1 4.6 pad_maximum_fusion.2
  743.8 14.5 %fusion.81 = f32[256,64,128]{0,1,2:T(8,128)} fusion(f32[2,128,64,256]{3,1,2,0:T(8,128)S(1)} %pad_maximum_fusion.2, f32[1,64,64]{2,1,0:T(8,128)S(1)} %fusion.125, f32[1,64,64]{2,1,0:T(8,128)S(1)} %copy-done), kind=kOutput, calls=%fused_computation.142 | convolution fusion | flops 1610629120 | bytes 25198592 | tf_op jit(solution)/shard_map/cbp,capy->yba/dot_general | solution.py:83
  758.3 11.5 %copy.115 = f32[256,64,128]{0,2,1:T(8,128)} copy(f32[256,64,128]{0,1,2:T(8,128)} %fusion.81) | data formatting | bytes 16777216 | tf_op jit(solution)/shard_map/cbp,capy->yba/transpose | solution.py:83
  769.8 8.9 %copy.116 = f32[256,8192]{1,0:T(8,128)} copy(f32[256,8192]{0,1:T(8,128)} %bitcast.258) | data formatting | bytes 16777216 | tf_op jit(solution)/shard_map/reshape | solution.py:84
  (163 shorter events, 13.9 us)
Async XLA Ops:
  1.4 9.7 %all-to-all-start = ((s32[4,1,128]{2,1,0:T(1,128)}), s32[4,1,128]{2,1,0:T(1,128)S(1)}, u32[]{:S(2)}, u32[]{:S(2)}) async-start(s32[4,1,128]{2,1,0:T(1,128)} %reshape.440), calls=%async_computation | async-start | bytes 4096 | tf_op jit(solution)/shard_map/all_to_all | solution.py:153
  11.1 10.5 %all-to-all-start.1 = ((f32[4,4,32,2,128]{4,2,3,1,0:T(8,128)}), f32[4,4,32,2,128]{4,2,3,1,0:T(8,128)S(1)}, u32[]{:S(2)}, u32[]{:S(2)}) async-start(f32[4,4,32,2,128]{4,2,3,1,0:T(8,128)} %bitcast.32), calls=%async_computation.1 | async-start | bytes 1048576 | tf_op jit(solution)/shard_map/all_to_all | solution.py:138
  21.5 10.0 %all-to-all-start.2 = ((s32[4,4,32,2,128]{4,2,3,1,0:T(8,128)}), s32[4,4,32,2,128]{4,2,3,1,0:T(8,128)S(1)}, u32[]{:S(2)}, u32[]{:S(2)}) async-start(s32[4,4,32,2,128]{4,2,3,1,0:T(8,128)} %bitcast.36), calls=%async_computation.2 | async-start | bytes 1048576 | tf_op jit(solution)/shard_map/all_to_all | solution.py:146
  31.6 152.5 %copy-start = (f32[1,64,64]{2,1,0:T(8,128)S(1)}, f32[1,64,64]{2,1,0:T(8,128)}, u32[]{:S(2)}) copy-start(f32[1,64,64]{2,1,0:T(8,128)} %get-tuple-element.149) | copy-start | bytes 49156
  31.6 152.5 %copy-start.1 = (f32[1,64,64]{2,1,0:T(8,128)S(1)}, f32[1,64,64]{2,1,0:T(8,128)}, u32[]{:S(2)}) copy-start(f32[1,64,64]{2,1,0:T(8,128)} %get-tuple-element.148) | copy-start | bytes 49156
  180.0 19.3 %collective-permute-start = (f32[64,2,8,128]{3,0,1,2:T(8,128)S(1)}, f32[64,2,8,128]{3,0,1,2:T(8,128)S(1)}, u32[]{:S(2)}, u32[]{:S(2)}) collective-permute-start(f32[64,2,8,128]{3,0,1,2:T(8,128)S(1)} %slice_bitcast_fusion.7), channel_id=1, source_target_pairs={{0,1},{1,2},{2,3},{3,4},{4,5},{5,6},{6,7},{7,8},{8,9},{9,10},{10,1... | collective-permute-start | bytes 1572872 | tf_op jit(solution)/shard_map/ppermute | solution.py:19
  201.3 13.5 %copy-start.2 = (f32[64,128]{1,0:T(8,128)S(1)}, f32[64,128]{1,0:T(8,128)}, u32[]{:S(2)}) copy-start(f32[64,128]{1,0:T(8,128)} %get-tuple-element.150) | copy-start | bytes 98308
  201.3 13.5 %copy-start.3 = (f32[64,128]{1,0:T(8,128)S(1)}, f32[64,128]{1,0:T(8,128)}, u32[]{:S(2)}) copy-start(f32[64,128]{1,0:T(8,128)} %get-tuple-element.151) | copy-start | bytes 98308
  304.1 387.9 %all-to-all-start.3 = ((f32[2,256,32,256]{3,1,0,2:T(8,128)}), f32[2,256,32,256]{3,1,0,2:T(8,128)}, u32[]{:S(2)}, u32[]{:S(2)}) async-start(f32[2,256,32,256]{3,1,0,2:T(8,128)} %copy.111), calls=%async_computation.3 | async-start | bytes 33554432 | tf_op jit(solution)/shard_map/all_to_all | solution.py:176
